TPU v7x, 32 devices: a whole 2x2x4 slice. The times are simulated.
32 devices in a mesh: heads: 2 (over core), blk: 16 (over z, y, x).
Axes of the slice: x: 2, y: 2, z: 4, core: 2. Of those that a mesh axis runs over, the one named last changes fastest.
Arguments:
- queries: bfloat16 [3072, 4096], P('blk', 'heads'), may hold values from -8 to 8
- keys: bfloat16 [3072, 4096], P('blk', 'heads'), may hold values from -6 to 6
- values: bfloat16 [3072, 4096], P('blk', 'heads'), may hold values from -24 to 24
- prefix_keys: bfloat16 [1024, 4096], P('blk', 'heads'), may hold values from -8 to 8
- prefix_values: bfloat16 [1024, 4096], P('blk', 'heads'), may hold values from -24 to 24
- lengths: int32 [24], replicated, may hold values from 1 to 224, 3072 in all
- groups: int32 [24], replicated, may hold values from 0 to 3, as said below
- out_weight: bfloat16 [4096, 4096], P('heads'), may hold values from -0.09375 to 0.09375
Outputs:
- attn_branch: bfloat16 [3072, 4096], P('blk', 'heads')
Inputs may be any that keep to these rules, and one draw needn't show every extreme that they name: Each of the 4 groups holds 6 requests. The lengths sum to 3072; the longest is 224.
All inputs are finite; a program needn't handle non-finite values.
Results may differ from a plain program's by a relative error of at most 0.019.
Values may be sent and summed in bfloat16 or wider, within the bound.
A program may use at most 128 MiB of HBM per device.

v0:
```python
import math

import jax
import jax.numpy as jnp
from jax import lax
from jax.sharding import PartitionSpec as P

HD = 128
ROT = 32
GROUPS = 4
MOST = 224


def shifted(block, axis, distance):
    devices = range(lax.axis_size(axis))
    route = [(i - distance, i) for i in devices if i - distance in devices]
    return lax.ppermute(block, axis, route)


def token_tables(lengths, groups, tok_index, prefix_len):
    ends = jnp.cumsum(lengths)
    starts = ends - lengths
    inside = (starts[None, :] <= tok_index[:, None]) & (tok_index[:, None] < ends[None, :])
    start_tok = jnp.sum(jnp.where(inside, starts[None, :] + 1, 0), axis=1) - 1
    group_tok = jnp.sum(jnp.where(inside, groups[None, :], 0), axis=1)
    position = prefix_len + tok_index - start_tok
    return (start_tok, group_tok, position)


def rotary(field, position):
    half = ROT // 2
    inverse = 10000.0 ** (-(jnp.arange(half, dtype=jnp.float32) * 2.0 / ROT))
    angle = position.astype(jnp.float32)[:, None] * inverse[None, :]
    angle = jnp.concatenate([angle, angle], axis=1)
    cosine = jnp.cos(angle)[:, None, :]
    sine = jnp.sin(angle)[:, None, :]
    front = field[..., :ROT]
    turned = jnp.concatenate([-front[..., half:], front[..., :half]], axis=-1)
    rotated = front * cosine + turned * sine
    return jnp.concatenate([rotated, field[..., ROT:]], axis=-1)


def online_update(state, q_rot, key_rows, value_rows, mask, scale):
    top_old, total_old, accum_old = state
    score = jnp.einsum("qhd,khd->hqk", q_rot, key_rows, preferred_element_type=jnp.float32) * scale
    score = jnp.where(mask[None], score, -1e30)
    top_new = jnp.maximum(top_old, jnp.max(score, axis=-1))
    expo = jnp.exp(score - top_new[..., None])
    factor = jnp.exp(top_old - top_new)
    total_new = total_old * factor + jnp.sum(expo, axis=-1)
    weights = expo.astype(jnp.bfloat16)
    accum_new = accum_old * factor[..., None] + jnp.einsum(
        "hqk,khd->hqd", weights, value_rows, preferred_element_type=jnp.float32
    )
    return (top_new, total_new, accum_new)


def body(queries, keys, values, prefix_keys, prefix_values, lengths, groups, out_weight):
    tok = queries.shape[0]
    width = queries.shape[1]
    heads_dev = width // HD
    scale = 1.0 / math.sqrt(HD)
    n_blk = lax.axis_size("blk")
    prefix_len = prefix_keys.shape[0] * n_blk // GROUPS
    first = lax.axis_index("blk") * tok
    tok_index = first + jnp.arange(tok, dtype=jnp.int32)
    start_tok, group_tok, position = token_tables(lengths, groups, tok_index, prefix_len)
    q_rot = rotary(queries.reshape(tok, heads_dev, HD).astype(jnp.float32), position).astype(
        jnp.bfloat16
    )
    k_rot = rotary(keys.reshape(tok, heads_dev, HD).astype(jnp.float32), position).astype(
        jnp.bfloat16
    )
    v_own = values.reshape(tok, heads_dev, HD)
    span = (MOST - 2) // tok + 1
    key_list = [k_rot]
    value_list = [v_own]
    index_list = [tok_index]
    for distance in range(1, span + 1):
        moved_k, moved_v = shifted((k_rot, v_own), "blk", distance)
        key_list = [moved_k] + key_list
        value_list = [moved_v] + value_list
        index_list = [tok_index - distance * tok] + index_list
    near_k = jnp.concatenate(key_list, axis=0)
    near_v = jnp.concatenate(value_list, axis=0)
    near_index = jnp.concatenate(index_list, axis=0)
    near_start = token_tables(lengths, groups, near_index, prefix_len)[0]
    near_mask = (near_start[None, :] == start_tok[:, None]) & (
        near_index[None, :] <= tok_index[:, None]
    )
    state = (
        jnp.full((heads_dev, tok), -1e30, jnp.float32),
        jnp.zeros((heads_dev, tok), jnp.float32),
        jnp.zeros((heads_dev, tok, HD), jnp.float32),
    )
    state = online_update(state, q_rot, near_k, near_v, near_mask, scale)
    piece_k = lax.all_gather(prefix_keys, "blk", axis=0, tiled=True)
    piece_v = lax.all_gather(prefix_values, "blk", axis=0, tiled=True)
    count = piece_k.shape[0]
    row_group = jnp.arange(count, dtype=jnp.int32) // prefix_len
    mask = row_group[None, :] == group_tok[:, None]
    top_final, total_final, accum_final = online_update(
        state,
        q_rot,
        piece_k.reshape(count, heads_dev, HD),
        piece_v.reshape(count, heads_dev, HD),
        mask,
        scale,
    )
    attn = accum_final / total_final[..., None]
    attn = jnp.transpose(attn, (1, 0, 2)).reshape(tok, width).astype(jnp.bfloat16)
    partial_out = jnp.dot(attn, out_weight, preferred_element_type=jnp.float32)
    projected = lax.psum_scatter(
        partial_out.astype(jnp.bfloat16), "heads", scatter_dimension=1, tiled=True
    )
    return projected


def solution(mesh):
    placed = (
        P("blk", "heads"),
        P("blk", "heads"),
        P("blk", "heads"),
        P("blk", "heads"),
        P("blk", "heads"),
        P(),
        P(),
        P("heads", None),
    )
    return jax.shard_map(
        body, mesh=mesh, in_specs=placed, out_specs=P("blk", "heads"), check_vma=False
    )
```

profile of v0, /device:TPU:26, one launch (start us, length us, event | category | flops | bytes accessed | tf_op | source)
XLA Modules:
  0.0 261.2 jit_solution(15285865329272532625)
XLA Ops:
  6.5 0.0 copy-start
  6.5 0.0 copy-start.4
  6.5 0.0 all-gather.3.cloned.1.call-start
  6.5 0.7 all-gather.3.cloned.1.call-update
  7.3 0.0 all-gather.5.cloned.1.call-start
  7.3 0.7 all-gather.5.cloned.1.call-update
  8.0 0.0 reduce-scatter.2.cloned.1.call-start
  8.1 0.7 copy.44
  8.8 0.1 reduce
  9.0 0.7 broadcast_add_fusion.2
  9.6 0.7 select_reduce_fusion.1
  10.4 0.1 broadcast_multiply_fusion
  10.5 0.1 fusion.51
  10.6 0.1 copy.46
  10.7 0.1 copy.47
  10.8 0.0 copy-done
  10.8 0.3 fusion.70
  11.1 0.3 slice.45
  11.4 0.0 copy-done.4
  11.4 0.3 fusion.69
  11.6 1.2 slice_negate_fusion
  12.8 0.0 copy-start.3
  12.8 1.0 fusion.32
  13.8 0.4 pad_maximum_fusion.1
  14.3 3.4 %collective-permute-start = (bf16[192,16,128]{2,0,1:T(8,128)(2,1)S(1)}, bf16[192,16,128]{2,0,1:T(8,128)(2,1)S(1)}, u32[]{:S(2)}, u32[]{:S(2)}) collective-permute-start(bf16[192,16,128]{2,0,1:T(8,128)(2,1)S(1)} %pad_maximum_fusion.1), channel_id=1, source_target_pairs={{0,2},{1,3},{2,4},{3,5},{4,6},{5,7},{6,8},{7,9},{8,10},{9,11},{10,... | collective-permute-start | bytes 2359304 | tf_op jit(solution)/shard_map/ppermute | solution.py:17
  17.7 1.9 collective-permute-start.1
  19.6 0.0 copy-done.3
  19.6 0.2 copy_bitcast_fusion
  19.8 1.9 collective-permute-start.2
  21.8 2.3 collective-permute-start.3
  24.1 0.3 slice.41
  24.4 0.1 pad_add_fusion
  24.5 0.1 select_reduce_fusion
  24.6 0.2 compare_and_fusion
  24.8 0.2 broadcast_compare_fusion
  24.9 18.1 %collective-permute-done = bf16[192,16,128]{2,0,1:T(8,128)(2,1)S(1)} collective-permute-done((bf16[192,16,128]{2,0,1:T(8,128)(2,1)S(1)}, bf16[192,16,128]{2,0,1:T(8,128)(2,1)S(1)}, u32[]{:S(2)}, u32[]{:S(2)}) %collective-permute-start) | collective-permute-done | bytes 786464 | tf_op jit(solution)/shard_map/ppermute | solution.py:17
  43.1 0.0 collective-permute-done.1
  43.1 4.8 %fusion.3 = (f32[16,192]{1,0:T(8,128)S(1)}, f32[16,192,576]{2,1,0:T(8,128)}) fusion(pred[192,576]{1,0:T(8,128)(4,1)S(1)} %compare_and_fusion, bf16[192,16,96]{2,0,1:T(8,128)(2,1)S(1)} %slice.45, bf16[192,16,32]{2,0,1:T(8,128)(2,1)S(1)} %get-tuple-element.19, bf16[192,16,128]{2,0,1:T(8,128)(2,1)S(1)} %collective-permute-done.1, ...), kind=kOutput, calls=%fused_computation.7 | convolution fusion | flops 469300224 | bytes 10346496 | tf_op jit(solution)/shard_map/qhd,khd->hqk/dot_general | solution.py:45
  47.9 80.3 %all-gather.3.cloned.1.call-done = bf16[1024,2048]{1,0:T(8,128)(2,1)} async-done(((bf16[64,2048]{1,0:T(8,128)(2,1)}), bf16[1024,2048]{1,0:T(8,128)(2,1)}) %all-gather.3.cloned.1.call-update) | async-done | bytes 4194320 | tf_op jit(solution)/shard_map/all_gather | solution.py:97
  128.2 6.4 %copy.54 = bf16[1024,2048]{0,1:T(8,128)(2,1)} copy(bf16[1024,2048]{1,0:T(8,128)(2,1)} %all-gather.3.cloned.1.call-done) | data formatting | bytes 8388608 | tf_op jit(solution)/shard_map/all_gather | solution.py:97
  134.6 0.0 slice-start
  134.6 0.0 slice-start.1
  134.6 5.1 %fusion = (f32[16,192]{1,0:T(8,128)S(1)}, f32[16,192,1024]{2,1,0:T(8,128)S(1)}) fusion(pred[192,1024]{1,0:T(8,128)(4,1)S(1)} %broadcast_compare_fusion, bf16[1024,16,128]{0,2,1:T(8,128)(2,1)} %bitcast.67, bf16[192,16,96]{2,0,1:T(8,128)(2,1)S(1)} %slice.41, bf16[192,16,32]{2,0,1:T(8,128)(2,1)S(1)} %get-tuple-element.20), kind=kOutput, calls=%fused_computation.2 | convolution fusion | flops 816313344 | bytes 17772544 | tf_op jit(solution)/shard_map/qhd,khd->hqk/dot_general | solution.py:45
  139.7 0.0 copy-start.2
  139.7 0.0 slice-done
  139.8 0.0 slice-done.1
  139.8 2.3 fusion.10
  142.1 3.6 %fusion.1 = f32[16,192]{1,0:T(8,128)S(1)} fusion(f32[16,192,1024]{2,1,0:T(8,128)S(1)} %get-tuple-element.31, f32[16,192]{1,0:T(8,128)S(1)} %get-tuple-element.23, pred[192,1024]{1,0:T(8,128)(4,1)S(1)} %broadcast_compare_fusion), kind=kLoop, calls=%fused_computation.3 | loop fusion | flops 12579840 | bytes 12804096 | tf_op jit(solution)/shard_map/reduce_sum | solution.py:50
  145.7 0.0 copy-done.2
  145.7 69.0 %all-gather.5.cloned.1.call-done = bf16[1024,2048]{1,0:T(8,128)(2,1)} async-done(((bf16[64,2048]{1,0:T(8,128)(2,1)}), bf16[1024,2048]{1,0:T(8,128)(2,1)}) %all-gather.5.cloned.1.call-update) | async-done | bytes 4194320 | tf_op jit(solution)/shard_map/all_gather | solution.py:98
  214.7 6.3 %copy.56 = bf16[1024,2048]{0,1:T(8,128)(2,1)} copy(bf16[1024,2048]{1,0:T(8,128)(2,1)} %all-gather.5.cloned.1.call-done) | data formatting | bytes 8388608 | tf_op jit(solution)/shard_map/all_gather | solution.py:98
  221.1 7.6 %fusion.4 = f32[16,192,128]{2,1,0:T(8,128)S(1)} fusion(bf16[1024,16,128]{0,2,1:T(8,128)(2,1)} %bitcast.70, f32[16,192,1024]{2,1,0:T(8,128)} %copy-done.2, f32[16,192]{1,0:T(8,128)S(1)} %get-tuple-element.23, pred[192,1024]{1,0:T(8,128)(4,1)S(1)} %broadcast_compare_fusion), kind=kOutput, calls=%fused_computation.8 | convolution fusion | flops 817889280 | bytes 18558976 | tf_op jit(solution)/shard_map/hqk,khd->hqd/dot_general | solution.py:52
  228.7 0.0 collective-permute-done.2
  228.7 0.0 collective-permute-done.3
  228.7 5.8 %fusion.42 = bf16[16,24,8,128]{3,2,1,0:T(8,128)(2,1)S(1)} fusion(f32[16,192,128]{2,1,0:T(8,128)S(1)} %fusion.4, bf16[192,16,128]{2,0,1:T(8,128)(2,1)S(1)} %copy_bitcast_fusion, bf16[192,16,128]{2,0,1:T(8,128)(2,1)} %collective-permute-done.3, bf16[192,16,128]{2,0,1:T(8,128)(2,1)} %collective-permute-done.2, f32[16,192,576]{2,1,0:T(8,128)} %get-tuple-element.29, ...), kind=kOutput, calls=%fused_computation.49 | convolution fusion | flops 469106688 | bytes 11956224 | tf_op jit(solution)/shard_map/hqk,khd->hqd/dot_general | solution.py:52
  234.5 0.0 copy-start.1
  234.5 10.6 %convolution_convert_fusion = bf16[192,4096]{1,0:T(8,128)(2,1)} fusion(bf16[2048,4096]{1,0:T(8,128)(2,1)} %param.15, bf16[16,24,8,128]{3,2,1,0:T(8,128)(2,1)S(1)} %fusion.42), kind=kOutput, calls=%fused_computation.15 | convolution fusion | flops 3222011904 | bytes 19136512 | tf_op jit(solution)/shard_map/dot_general | solution.py:112
  245.1 0.0 reduce-scatter.2.cloned.1.call-update
  245.1 9.6 %reduce-scatter.2.cloned.1.call-done = bf16[192,2048]{1,0:T(8,128)(2,1)} async-done(((bf16[192,4096]{1,0:T(8,128)(2,1)}), bf16[192,2048]{1,0:T(8,128)(2,1)}) %reduce-scatter.2.cloned.1.call-update) | async-done | bytes 786448 | tf_op jit(solution)/shard_map/reduce_scatter | solution.py:113
  254.7 0.0 copy-done.1
  (10 shorter events, 0.1 us)
Async XLA Ops:
  6.5 4.2 %copy-start = (bf16[192,2048]{1,0:T(8,128)(2,1)S(1)}, bf16[192,2048]{1,0:T(8,128)(2,1)}, u32[]{:S(2)}) copy-start(bf16[192,2048]{1,0:T(8,128)(2,1)} %param.9) | copy-start | bytes 2359300
  6.5 4.8 %copy-start.4 = (bf16[192,2048]{1,0:T(8,128)(2,1)S(1)}, bf16[192,2048]{1,0:T(8,128)(2,1)}, u32[]{:S(2)}) copy-start(bf16[192,2048]{1,0:T(8,128)(2,1)} %param.8) | copy-start | bytes 2359300
  6.5 121.6 %all-gather.3.cloned.1.call-start = ((), (), s32[]{:S(2)}) async-start(), calls=%async_computation.1 | async-start | bytes 4456448 | tf_op jit(solution)/shard_map/all_gather | solution.py:97
  7.3 207.5 %all-gather.5.cloned.1.call-start = ((), (), s32[]{:S(2)}) async-start(), calls=%async_computation.2 | async-start | bytes 4456448 | tf_op jit(solution)/shard_map/all_gather | solution.py:98
  8.0 246.7 %reduce-scatter.2.cloned.1.call-start = ((), (), s32[]{:S(2)}) async-start(), calls=%async_computation.3 | async-start | bytes 2359296 | tf_op jit(solution)/shard_map/reduce_scatter | solution.py:113
  12.8 6.8 %copy-start.3 = (bf16[192,2048]{1,0:T(8,128)(2,1)S(1)}, bf16[192,2048]{1,0:T(8,128)(2,1)}, u32[]{:S(2)}) copy-start(bf16[192,2048]{1,0:T(8,128)(2,1)} %param.10) | copy-start | bytes 2359300
  14.3 28.8 %collective-permute-start = (bf16[192,16,128]{2,0,1:T(8,128)(2,1)S(1)}, bf16[192,16,128]{2,0,1:T(8,128)(2,1)S(1)}, u32[]{:S(2)}, u32[]{:S(2)}) collective-permute-start(bf16[192,16,128]{2,0,1:T(8,128)(2,1)S(1)} %pad_maximum_fusion.1), channel_id=1, source_target_pairs={{0,2},{1,3},{2,4},{3,5},{4,6},{5,7},{6,8},{7,9},{8,10},{9,11},{10,... | collective-permute-start | bytes 2359304 | tf_op jit(solution)/shard_map/ppermute | solution.py:17
  17.7 25.4 %collective-permute-start.1 = (bf16[192,16,128]{2,0,1:T(8,128)(2,1)S(1)}, bf16[192,16,128]{2,0,1:T(8,128)(2,1)S(1)}, u32[]{:S(2)}, u32[]{:S(2)}) collective-permute-start(bf16[192,16,128]{2,0,1:T(8,128)(2,1)S(1)} %pad_maximum_fusion.1), channel_id=1, source_target_pairs={{0,1},{1,2},{2,3},{3,4},{4,5},{5,6},{6,7},{7,8},{8,9},{9,10},{10,1... | collective-permute-start | bytes 2359304 | tf_op jit(solution)/shard_map/ppermute | solution.py:17
  19.8 208.8 %collective-permute-start.2 = (bf16[192,16,128]{2,0,1:T(8,128)(2,1)S(1)}, bf16[192,16,128]{2,0,1:T(8,128)(2,1)}, u32[]{:S(2)}, u32[]{:S(2)}) collective-permute-start(bf16[192,16,128]{2,0,1:T(8,128)(2,1)S(1)} %copy_bitcast_fusion), channel_id=1, source_target_pairs={{0,2},{1,3},{2,4},{3,5},{4,6},{5,7},{6,8},{7,9},{8,10},{9,11},{10,... | collective-permute-start | bytes 2359304 | tf_op jit(solution)/shard_map/ppermute | solution.py:17
  21.8 206.9 %collective-permute-start.3 = (bf16[192,16,128]{2,0,1:T(8,128)(2,1)S(1)}, bf16[192,16,128]{2,0,1:T(8,128)(2,1)}, u32[]{:S(2)}, u32[]{:S(2)}) collective-permute-start(bf16[192,16,128]{2,0,1:T(8,128)(2,1)S(1)} %copy_bitcast_fusion), channel_id=1, source_target_pairs={{0,1},{1,2},{2,3},{3,4},{4,5},{5,6},{6,7},{7,8},{8,9},{9,10},{10,1... | collective-permute-start | bytes 2359304 | tf_op jit(solution)/shard_map/ppermute | solution.py:17
  134.6 5.1 %slice-start = ((s8[7864320]{0:T(1024)(128)(4,1)}), s8[4194304]{0:T(1024)(128)(4,1)S(1)}, s32[]{:S(2)}) async-start(s8[7864320]{0:T(1024)(128)(4,1)} %bitcast.68), calls=%async_computation.4 | async-start | bytes 8388608
  134.6 5.2 %slice-start.1 = ((s8[7864320]{0:T(1024)(128)(4,1)}), s8[3670016]{0:T(1024)(128)(4,1)S(1)}, s32[]{:S(2)}) async-start(s8[7864320]{0:T(1024)(128)(4,1)} %bitcast.68), calls=%async_computation.5 | async-start | bytes 7340032
  139.7 6.0 %copy-start.2 = (f32[16,192,1024]{2,1,0:T(8,128)}, f32[16,192,1024]{2,1,0:T(8,128)S(1)}, u32[]{:S(2)}) copy-start(f32[16,192,1024]{2,1,0:T(8,128)S(1)} %get-tuple-element.31) | copy-start | bytes 37748740
  234.5 20.2 %copy-start.1 = (bf16[192,2048]{1,0:T(8,128)(2,1)S(1)}, bf16[192,2048]{1,0:T(8,128)(2,1)}, u32[]{:S(2)}) copy-start(bf16[192,2048]{1,0:T(8,128)(2,1)} %param.9) | copy-start | bytes 2359300
Sparse Core Ops, SparseCore 0:
  10.1 117.9 all-gather.2
  130.9 83.7 all-gather.4
  245.3 9.3 reduce-scatter.1
where the time goes:
time: 263 us; the launch traced here: 261 us
  waiting for transfers between devices  178 us (68%)
  matrix products  33.9 us (13%)
  local copies, waits for them, and re-layouts  14.5 us (6%)
  between operations  13.4 us (5%)
  other arithmetic  11.3 us (4%)
  starting transfers between devices  9.64 us (4%)
    all_gather x1, waiting for transfers between devices, body(): piece_k = lax.all_gather(prefix_keys, 'blk', axis=0, tiled=True)  80.3 us
    all_gather x1, waiting for transfers between devices, body(): piece_v = lax.all_gather(prefix_values, 'blk', axis=0, tiled=True)  69 us
    ppermute x4, waiting for transfers between devices, shifted(): return lax.ppermute(block, axis, route)  18.2 us
    dot_general x2, matrix products, online_update(): jnp.einsum('hqk,khd->hqd', weights, value_rows, preferred_element_type=jn...  13.4 us
    dot_general x1, matrix products, body(): partial_out = jnp.dot(attn, out_weight, preferred_element_type=jnp.float32)  10.6 us
    dot_general x2, matrix products, online_update(): jnp.einsum('qhd,khd->hqk', q_rot, key_rows, preferred_element_type=jnp.fl...  9.91 us
    ppermute x4, starting transfers between devices, shifted(): return lax.ppermute(block, axis, route)  9.56 us
    reduce_scatter x1, waiting for transfers between devices, body(): lax.psum_scatter(partial_out.astype(jnp.bfloat16), 'heads', scatter_dimen...  9.55 us
  transfers between devices with their start and end apart: 7, of which 4 were waited for; matrix products, arithmetic and copies ran while one was open for 17% of the time, Pallas kernels for 0%

commit v1 on v0

v1 whole, which is shorter than its diff:
```python
import functools
import math

import jax
import jax.numpy as jnp
from jax import lax
from jax.experimental import pallas as pl
from jax.experimental.pallas import tpu as pltpu
from jax.sharding import PartitionSpec as P

HD = 128
ROT = 32
GROUPS = 4
MOST = 224
HALO = (MOST - 1 + 15) // 16 * 16
TILE = 256
MESH = pl.DeviceIdType.MESH


def request_tables(lengths, groups, index):
    ends = jnp.cumsum(lengths)
    starts = ends - lengths
    inside = (starts <= index[..., None]) & (index[..., None] < ends)
    start = jnp.sum(jnp.where(inside, starts + 1, 0), axis=-1) - 1
    group = jnp.sum(jnp.where(inside, groups, 0), axis=-1)
    return start, group


def rotary_tables(position):
    half = ROT // 2
    inverse = 10000.0 ** (-(jnp.arange(half, dtype=jnp.float32) * 2.0 / ROT))
    angle = position.astype(jnp.float32)[:, None] * inverse[None, :]
    cosine, sine = jnp.cos(angle), jnp.sin(angle)
    rest = jnp.zeros((position.shape[0], HD - ROT), jnp.float32)
    none = jnp.zeros_like(sine)
    same = jnp.concatenate([cosine, cosine, rest + 1.0], axis=1)
    below = jnp.concatenate([-sine, none, rest], axis=1)
    above = jnp.concatenate([none, sine, rest], axis=1)
    return jnp.stack([same, below, above])


def dot_t(a, b):
    return lax.dot_general(a, b, (((1,), (1,)), ((), ())), preferred_element_type=jnp.float32)


def kernel(
    part, n_line, n_heads,
    q_ref, k_ref, v_ref, pk_ref, pv_ref, rot_ref, qs_ref, qg_ref, ks_ref, w_ref,
    out_ref,
    q_turn, k_turn, q_all, k_all, v_all, pk_all, pv_all, sent, attn, weight, give, take, own,
    pre_s, pre_r, qkv_s, qkv_r, line_s, line_r, halo_s, halo_r, back_s, back_r, sum_s, sum_r, w_sem,
):
    tok, width = q_ref.shape
    cols = width // part
    rows_pre = pk_ref.shape[0]
    n_pre = pk_all.shape[0]
    prefix_len = n_pre // GROUPS
    out_w = out_ref.shape[1]
    blk = lax.axis_index("blk")
    head = lax.axis_index("heads")
    line = blk // part
    member = blk % part
    base = line * part

    fetch = pltpu.make_async_copy(w_ref, weight, w_sem)
    fetch.start()

    barrier = pltpu.get_barrier_semaphore()
    for j in range(1, part):
        pl.semaphore_signal(
            barrier, inc=1, device_id={"blk": base + (member + j) % part}, device_id_type=MESH
        )
    for j in range(1, n_line):
        pl.semaphore_signal(
            barrier, inc=1, device_id={"blk": (line + j) % n_line * part + member},
            device_id_type=MESH,
        )
    for j in range(1, n_heads):
        pl.semaphore_signal(
            barrier, inc=1, device_id={"heads": (head + j) % n_heads}, device_id_type=MESH
        )
    pl.semaphore_wait(barrier, part + n_line + n_heads - 3)

    def columns(m):
        return pl.ds(pl.multiple_of(m * cols, cols), cols)

    def to_plane(src, dst, row, rows, send, recv, j):
        peer = (member + j) % part
        copy = pltpu.make_async_remote_copy(
            src_ref=src.at[:, columns(peer)],
            dst_ref=dst.at[pl.ds(pl.multiple_of(row, 16), rows), :],
            send_sem=send, recv_sem=recv,
            device_id={"blk": base + peer}, device_id_type=MESH,
        )
        copy.start()
        return copy

    pre_row = blk * rows_pre
    pre = [
        to_plane(src, dst, pre_row, rows_pre, pre_s.at[i, j], pre_r.at[i, j], j)
        for i, (src, dst) in enumerate(((pk_ref, pk_all), (pv_ref, pv_all)))
        for j in range(1, part)
    ]
    tok_row = member * tok
    moved = [
        to_plane(v_ref, v_all, HALO + tok_row, tok, qkv_s.at[2, j], qkv_r.at[2, j], j)
        for j in range(1, part)
    ]
    own_pre = pl.ds(pl.multiple_of(pre_row, 16), rows_pre)
    pk_all[own_pre, :] = pk_ref[:, columns(member)]
    pv_all[own_pre, :] = pv_ref[:, columns(member)]

    same, below, above = rot_ref[0], rot_ref[1], rot_ref[2]

    def turn(src, dst):
        for h in range(width // HD):
            at = slice(h * HD, (h + 1) * HD)
            x = src[:, at].astype(jnp.float32)
            y = x * same + pltpu.roll(x, HD - ROT // 2, 1) * below + pltpu.roll(x, ROT // 2, 1) * above
            dst[:, at] = y.astype(jnp.bfloat16)

    turn(k_ref, k_turn)
    moved += [
        to_plane(k_turn, k_all, HALO + tok_row, tok, qkv_s.at[1, j], qkv_r.at[1, j], j)
        for j in range(1, part)
    ]

    for copy in pre:
        copy.wait_recv()
    here = pl.ds(pl.multiple_of(line * (part * rows_pre), 16), part * rows_pre)
    lines = []
    for j in range(1, n_line):
        peer = (line + j) % n_line * part + member
        for i, ref in enumerate((pk_all, pv_all)):
            copy = pltpu.make_async_remote_copy(
                src_ref=ref.at[here, :], dst_ref=ref.at[here, :],
                send_sem=line_s.at[i, j], recv_sem=line_r.at[i, j],
                device_id={"blk": peer}, device_id_type=MESH,
            )
            copy.start()
            lines.append(copy)

    turn(q_ref, q_turn)
    moved_q = [
        to_plane(q_turn, q_all, tok_row, tok, qkv_s.at[0, j], qkv_r.at[0, j], j)
        for j in range(1, part)
    ]
    q_all[pl.ds(pl.multiple_of(tok_row, 16), tok), :] = q_turn[:, columns(member)]
    own_kv = pl.ds(pl.multiple_of(HALO + tok_row, 16), tok)
    k_all[own_kv, :] = k_turn[:, columns(member)]
    v_all[own_kv, :] = v_ref[:, columns(member)]

    for copy in moved:
        copy.wait_recv()
    halos = [
        pltpu.make_async_remote_copy(
            src_ref=ref.at[pl.ds(part * tok, HALO), :], dst_ref=ref.at[pl.ds(0, HALO), :],
            send_sem=halo_s.at[i], recv_sem=halo_r.at[i],
            device_id={"blk": (line + 1) % n_line * part + member}, device_id_type=MESH,
        )
        for i, ref in enumerate((k_all, v_all))
    ]

    @pl.when(line < n_line - 1)
    def _():
        for copy in halos:
            copy.start()

    @pl.when(line == 0)
    def _():
        k_all[pl.ds(0, HALO), :] = jnp.zeros((HALO, cols), jnp.bfloat16)
        v_all[pl.ds(0, HALO), :] = jnp.zeros((HALO, cols), jnp.bfloat16)

    for copy in moved_q:
        copy.wait_recv()

    @pl.when(line > 0)
    def _():
        for copy in halos:
            copy.wait_recv()

    for copy in lines:
        copy.wait_recv()

    span = HALO + tok
    factor = math.log2(math.e) / math.sqrt(HD)
    later = lax.broadcasted_iota(jnp.int32, (tok, span), 1) - HALO <= lax.broadcasted_iota(
        jnp.int32, (tok, span), 0
    )

    def send_back(step):
        peer = (member + step) % part
        row = pl.ds(pl.multiple_of(peer * tok, 16), tok)
        return pltpu.make_async_remote_copy(
            src_ref=sent.at[row, :], dst_ref=attn.at[:, columns(member)],
            send_sem=back_s.at[step], recv_sem=back_r.at[step],
            device_id={"blk": base + peer}, device_id_type=MESH,
        )

    def block(step, carry):
        b = (member + step) % part
        row = pl.ds(pl.multiple_of(b * tok, 16), tok)
        window = pl.ds(pl.multiple_of(b * tok, 16), span)
        group = qg_ref[row, :]
        allowed = (ks_ref[b] == qs_ref[row, :]) & later
        for h in range(cols // HD):
            at = slice(h * HD, (h + 1) * HD)
            q = q_all[row, at]
            near = jnp.where(allowed, dot_t(q, k_all[window, at]), -1e30)
            far = dot_t(q, pk_all[0:prefix_len, at])
            for g in range(1, GROUPS):
                far = jnp.where(
                    group == g, dot_t(q, pk_all[g * prefix_len:(g + 1) * prefix_len, at]), far
                )
            top = jnp.maximum(
                jnp.max(near, axis=1, keepdims=True), jnp.max(far, axis=1, keepdims=True)
            )
            e_near = jnp.exp2((near - top) * factor)
            e_far = jnp.exp2((far - top) * factor)
            total = jnp.sum(e_near, axis=1, keepdims=True) + jnp.sum(e_far, axis=1, keepdims=True)
            acc = jnp.dot(
                e_near.astype(jnp.bfloat16), v_all[window, at], preferred_element_type=jnp.float32
            )
            for g in range(GROUPS):
                acc += jnp.dot(
                    jnp.where(group == g, e_far, 0.0).astype(jnp.bfloat16),
                    pv_all[g * prefix_len:(g + 1) * prefix_len, at],
                    preferred_element_type=jnp.float32,
                )
            sent[row, at] = (acc / total).astype(jnp.bfloat16)

        @pl.when(step < part)
        def _():
            send_back(step).start()

        return carry

    lax.fori_loop(1, part + 1, block, 0)
    attn[:, columns(member)] = sent[pl.ds(pl.multiple_of(tok_row, 16), tok), :]
    for step in range(1, part):
        send_back(step).wait_recv()
    fetch.wait()

    def project(first, t):
        at = pl.ds(pl.multiple_of(first + t * TILE, TILE), TILE)
        return jnp.dot(attn[...], weight[:, at], preferred_element_type=jnp.float32)

    sums = []
    for j in range(1, n_heads):
        peer = (head + j) % n_heads

        @pl.loop(0, out_w // TILE)
        def _(t):
            at = pl.ds(pl.multiple_of(t * TILE, TILE), TILE)
            give[j - 1, :, at] = project(peer * out_w, t).astype(jnp.bfloat16)

        copy = pltpu.make_async_remote_copy(
            src_ref=give.at[j - 1], dst_ref=take.at[j - 1],
            send_sem=sum_s.at[j], recv_sem=sum_r.at[j],
            device_id={"heads": peer}, device_id_type=MESH,
        )
        copy.start()
        sums.append(copy)

    @pl.loop(0, out_w // TILE)
    def _(t):
        at = pl.ds(pl.multiple_of(t * TILE, TILE), TILE)
        own[:, at] = project(head * out_w, t)

    for copy in sums:
        copy.wait_recv()

    @pl.loop(0, out_w // TILE)
    def _(t):
        at = pl.ds(pl.multiple_of(t * TILE, TILE), TILE)
        whole = own[:, at]
        for j in range(1, n_heads):
            whole += take[j - 1, :, at].astype(jnp.float32)
        out_ref[:, at] = whole.astype(jnp.bfloat16)

    for copy in pre + moved + lines + moved_q + sums:
        copy.wait_send()
    for step in range(1, part):
        send_back(step).wait_send()

    @pl.when(line < n_line - 1)
    def _():
        for copy in halos:
            copy.wait_send()


def body(queries, keys, values, prefix_keys, prefix_values, lengths, groups, out_weight):
    tok, width = queries.shape
    rows_pre = prefix_keys.shape[0]
    n_blk = lax.axis_size("blk")
    n_heads = lax.axis_size("heads")
    part = math.gcd(4, math.gcd(width // HD, n_blk))
    n_line = n_blk // part
    cols = width // part
    n_pre = rows_pre * n_blk
    out_w = out_weight.shape[1] // n_heads
    blk = lax.axis_index("blk")
    first = blk // part * (part * tok)
    plane = first + jnp.arange(part * tok, dtype=jnp.int32)
    start, group = request_tables(lengths, groups, plane)
    window = (
        first - HALO
        + jnp.arange(part, dtype=jnp.int32)[:, None, None] * tok
        + jnp.arange(HALO + tok, dtype=jnp.int32)[None, None, :]
    )
    near_start = request_tables(lengths, groups, window)[0]
    mine = blk * tok + jnp.arange(tok, dtype=jnp.int32)
    position = n_pre // GROUPS + mine - request_tables(lengths, groups, mine)[0]
    tables = rotary_tables(position)
    vmem = pl.BlockSpec(memory_space=pltpu.VMEM)
    bf = jnp.bfloat16
    dma = pltpu.SemaphoreType.DMA
    return pl.pallas_call(
        functools.partial(kernel, part, n_line, n_heads),
        out_shape=jax.ShapeDtypeStruct((tok, out_w), bf),
        in_specs=[vmem] * 9 + [pl.BlockSpec(memory_space=pl.ANY)],
        out_specs=vmem,
        scratch_shapes=[
            pltpu.VMEM((tok, width), bf),
            pltpu.VMEM((tok, width), bf),
            pltpu.VMEM((part * tok, cols), bf),
            pltpu.VMEM((HALO + part * tok, cols), bf),
            pltpu.VMEM((HALO + part * tok, cols), bf),
            pltpu.VMEM((n_pre, cols), bf),
            pltpu.VMEM((n_pre, cols), bf),
            pltpu.VMEM((part * tok, cols), bf),
            pltpu.VMEM((tok, width), bf),
            pltpu.VMEM(out_weight.shape, bf),
            pltpu.VMEM((n_heads - 1, tok, out_w), bf),
            pltpu.VMEM((n_heads - 1, tok, out_w), bf),
            pltpu.VMEM((tok, out_w), jnp.float32),
            dma((2, part)), dma((2, part)),
            dma((3, part)), dma((3, part)),
            dma((2, n_line)), dma((2, n_line)),
            dma((2,)), dma((2,)),
            dma((part,)), dma((part,)),
            dma((n_heads,)), dma((n_heads,)),
            dma,
        ],
        compiler_params=pltpu.CompilerParams(
            collective_id=0, has_side_effects=True, vmem_limit_bytes=56 << 20
        ),
    )(
        queries, keys, values, prefix_keys, prefix_values, tables,
        start[:, None], group[:, None], near_start, out_weight,
    )


def solution(mesh):
    placed = (
        P("blk", "heads"),
        P("blk", "heads"),
        P("blk", "heads"),
        P("blk", "heads"),
        P("blk", "heads"),
        P(),
        P(),
        P("heads", None),
    )
    return jax.shard_map(
        body, mesh=mesh, in_specs=placed, out_specs=P("blk", "heads"), check_vma=False
    )
```

time: 263 us -> 96.6 us (0.37)
  the two profiles are of different devices: /device:TPU:26 before, /device:TPU:18 now
where the time goes in v1:
time: 96.6 us; the launch traced here: 96.4 us
  Pallas kernels  87.7 us (91%)
  local copies, waits for them, and re-layouts  5.41 us (6%)
  other arithmetic  3.22 us (3%)
    pallas_call x1, Pallas kernels, body(): pl.pallas_call(functools.partial(kernel, part, n_line, n_heads), out_shap...  87.7 us
    unnamed x1, local copies, waits for them, and re-layouts  2.09 us

profile of v1, /device:TPU:18, one launch (start us, length us, event | category | flops | bytes accessed | tf_op | source)
XLA Modules:
  0.0 96.4 jit_solution(16158907596546096580)
XLA Ops:
  0.0 0.1 pad.11.clone
  0.1 0.1 pad.8.clone
  0.2 0.1 iota_add_fusion
  0.3 0.7 copy.13
  1.0 0.1 reduce.1
  1.2 0.7 broadcast_add_fusion.2
  1.8 0.1 select_reduce_fusion
  2.0 0.6 sub.43.ks_ref
  2.6 0.1 select_reduce_fusion.3
  2.7 0.8 select_reduce_fusion.1
  3.4 0.4 multiply_cosine_fusion
  3.9 0.1 maximum_bitcast_fusion.1
  4.0 0.7 pad_maximum_fusion.rot_ref
  4.8 0.9 sub.44.qs_ref
  5.7 0.9 broadcast_in_dim.64.qg_ref
  6.6 87.7 %shard_map.82 = bf16[192,2048]{1,0:T(8,128)(2,1)} custom-call(bf16[192,2048]{1,0:T(8,128)(2,1)} %q_ref.1, bf16[192,2048]{1,0:T(8,128)(2,1)} %k_ref.1, bf16[192,2048]{1,0:T(8,128)(2,1)} %v_ref.1, bf16[64,2048]{1,0:T(8,128)(2,1)} %pk_ref.1, bf16[64,2048]{1,0:T(8,128)(2,1)} %pv_ref.1, f32[3,192,128]{2,1,0:T(8,128)} %pad_maximum_fusion.rot_ref, ...), custom_call_target="tpu_custom_call" | custom-call | tf_op jit(solution)/shard_map/pallas_call | solution.py:318
  94.3 2.1 %copy.17 = bf16[192,2048]{1,0:T(8,128)(2,1)} copy(bf16[192,2048]{1,0:T(8,128)(2,1)} %shard_map.82) | data formatting | bytes 1572864
  (11 shorter events, 0.1 us)

commit v2 on v1

--- a/solution.py
+++ b/solution.py
@@ -3,6 +3,7 @@
 
 import jax
 import jax.numpy as jnp
+import numpy as np
 from jax import lax
 from jax.experimental import pallas as pl
 from jax.experimental.pallas import tpu as pltpu
@@ -17,26 +18,12 @@
 MESH = pl.DeviceIdType.MESH
 
 
-def request_tables(lengths, groups, index):
-    ends = jnp.cumsum(lengths)
-    starts = ends - lengths
-    inside = (starts <= index[..., None]) & (index[..., None] < ends)
-    start = jnp.sum(jnp.where(inside, starts + 1, 0), axis=-1) - 1
-    group = jnp.sum(jnp.where(inside, groups, 0), axis=-1)
-    return start, group
-
-
-def rotary_tables(position):
+def rotary_rates():
     half = ROT // 2
-    inverse = 10000.0 ** (-(jnp.arange(half, dtype=jnp.float32) * 2.0 / ROT))
-    angle = position.astype(jnp.float32)[:, None] * inverse[None, :]
-    cosine, sine = jnp.cos(angle), jnp.sin(angle)
-    rest = jnp.zeros((position.shape[0], HD - ROT), jnp.float32)
-    none = jnp.zeros_like(sine)
-    same = jnp.concatenate([cosine, cosine, rest + 1.0], axis=1)
-    below = jnp.concatenate([-sine, none, rest], axis=1)
-    above = jnp.concatenate([none, sine, rest], axis=1)
-    return jnp.stack([same, below, above])
+    rates = np.zeros((1, HD), np.float32)
+    rates[0, :half] = 10000.0 ** (-(np.arange(half, dtype=np.float32) * np.float32(2.0 / ROT)))
+    rates[0, half:ROT] = rates[0, :half]
+    return rates
 
 
 def dot_t(a, b):
@@ -45,17 +32,21 @@
 
 def kernel(
     part, n_line, n_heads,
-    q_ref, k_ref, v_ref, pk_ref, pv_ref, rot_ref, qs_ref, qg_ref, ks_ref, w_ref,
-    out_ref,
-    q_turn, k_turn, q_all, k_all, v_all, pk_all, pv_all, sent, attn, weight, give, take, own,
-    pre_s, pre_r, qkv_s, qkv_r, line_s, line_r, halo_s, halo_r, back_s, back_r, sum_s, sum_r, w_sem,
+    len_ref, grp_ref, rate_ref, q_ref, k_ref, v_ref, pk_ref, pv_ref, w_ref,
+    own, take,
+    q_in, k_in, q_turn, k_turn, q_all, k_all, v_all, pk_all, pv_all, sent, attn, weight, give,
+    begin, group_of, near_begin,
+    pre_s, pre_r, qkv_s, qkv_r, line_s, line_r, halo_s, halo_r, back_s, back_r, sum_s, sum_r,
+    in_sem, own_sem, w_sem,
 ):
     tok, width = q_ref.shape
     cols = width // part
     rows_pre = pk_ref.shape[0]
     n_pre = pk_all.shape[0]
     prefix_len = n_pre // GROUPS
-    out_w = out_ref.shape[1]
+    out_w = own.shape[1]
+    requests = len_ref.shape[0]
+    span = HALO + tok
     blk = lax.axis_index("blk")
     head = lax.axis_index("heads")
     line = blk // part
@@ -63,7 +54,12 @@
     base = line * part
 
     fetch = pltpu.make_async_copy(w_ref, weight, w_sem)
-    fetch.start()
+    loads = [
+        pltpu.make_async_copy(k_ref, k_in, in_sem.at[0]),
+        pltpu.make_async_copy(q_ref, q_in, in_sem.at[1]),
+    ]
+    for copy in loads:
+        copy.start()
 
     barrier = pltpu.get_barrier_semaphore()
     for j in range(1, part):
@@ -107,10 +103,41 @@
         for j in range(1, part)
     ]
     own_pre = pl.ds(pl.multiple_of(pre_row, 16), rows_pre)
-    pk_all[own_pre, :] = pk_ref[:, columns(member)]
-    pv_all[own_pre, :] = pv_ref[:, columns(member)]
-
-    same, below, above = rot_ref[0], rot_ref[1], rot_ref[2]
+    own_row = pl.ds(pl.multiple_of(tok_row, 16), tok)
+    own_kv = pl.ds(pl.multiple_of(HALO + tok_row, 16), tok)
+    local = [
+        pltpu.make_async_copy(pk_ref.at[:, columns(member)], pk_all.at[own_pre, :], own_sem.at[0]),
+        pltpu.make_async_copy(pv_ref.at[:, columns(member)], pv_all.at[own_pre, :], own_sem.at[1]),
+        pltpu.make_async_copy(v_ref.at[:, columns(member)], v_all.at[own_kv, :], own_sem.at[2]),
+    ]
+    for copy in local:
+        copy.start()
+    fetch.start()
+
+    def request(r, state, queries, near):
+        start, begins, owners, nears = state
+        length = len_ref[r]
+        end = start + length
+        inside = (queries >= start) & (queries < end)
+        begins = jnp.where(inside, start + 1, begins)
+        if owners is not None:
+            owners = jnp.where(inside, grp_ref[r], owners)
+        if nears is not None:
+            nears = jnp.where((near >= start) & (near < end), start + 1, nears)
+        return end, begins, owners, nears
+
+    index = blk * tok + lax.broadcasted_iota(jnp.int32, (tok, 1), 0)
+    zero = jnp.zeros((tok, 1), jnp.int32)
+    mine = lax.fori_loop(
+        0, requests, lambda r, state: request(r, state, index, None),
+        (jnp.int32(0), zero, None, None),
+    )[1]
+    position = prefix_len + index + 1 - mine
+    angle = position.astype(jnp.float32) * rate_ref[...]
+    lane = lax.broadcasted_iota(jnp.int32, (tok, HD), 1)
+    same, sine = jnp.cos(angle), jnp.sin(angle)
+    below = jnp.where(lane < ROT // 2, -sine, 0.0)
+    above = jnp.where(lane < ROT // 2, 0.0, sine)
 
     def turn(src, dst):
         for h in range(width // HD):
@@ -119,7 +146,8 @@
             y = x * same + pltpu.roll(x, HD - ROT // 2, 1) * below + pltpu.roll(x, ROT // 2, 1) * above
             dst[:, at] = y.astype(jnp.bfloat16)
 
-    turn(k_ref, k_turn)
+    loads[0].wait()
+    turn(k_in, k_turn)
     moved += [
         to_plane(k_turn, k_all, HALO + tok_row, tok, qkv_s.at[1, j], qkv_r.at[1, j], j)
         for j in range(1, part)
@@ -127,28 +155,55 @@
 
     for copy in pre:
         copy.wait_recv()
-    here = pl.ds(pl.multiple_of(line * (part * rows_pre), 16), part * rows_pre)
-    lines = []
-    for j in range(1, n_line):
-        peer = (line + j) % n_line * part + member
-        for i, ref in enumerate((pk_all, pv_all)):
-            copy = pltpu.make_async_remote_copy(
-                src_ref=ref.at[here, :], dst_ref=ref.at[here, :],
-                send_sem=line_s.at[i, j], recv_sem=line_r.at[i, j],
-                device_id={"blk": peer}, device_id_type=MESH,
-            )
-            copy.start()
-            lines.append(copy)
-
-    turn(q_ref, q_turn)
+    for copy in local[:2]:
+        copy.wait()
+    shard = part * rows_pre
+
+    def hop(sign, i, d):
+        ref = (pk_all, pv_all)[i]
+        side = (sign + 1) // 2
+        away = lax.rem(line - sign * (d - 1) + n_line, n_line)
+        rows = pl.ds(pl.multiple_of(away * shard, 16), shard)
+        return pltpu.make_async_remote_copy(
+            src_ref=ref.at[rows, :], dst_ref=ref.at[rows, :],
+            send_sem=line_s.at[side, i, d], recv_sem=line_r.at[side, i, d],
+            device_id={"blk": lax.rem(line + sign + n_line, n_line) * part + member},
+            device_id_type=MESH,
+        )
+
+    def sends(sign, d):
+        if sign > 0:
+            return (line >= d - 1) & (line < n_line - 1)
+        return (line < n_line - d + 1) & (line > 0)
+
+    def receives(sign, d):
+        return line >= d if sign > 0 else line < n_line - d
+
+    def forward(d):
+        for i in range(2):
+            for sign in (1, -1):
+                if d > 1:
+                    @pl.when(receives(sign, d - 1))
+                    def _():
+                        hop(sign, i, d - 1).wait_recv()
+
+                if d < n_line:
+                    @pl.when(sends(sign, d))
+                    def _():
+                        hop(sign, i, d).start()
+
+    forward(1)
+    loads[1].wait()
+    turn(q_in, q_turn)
     moved_q = [
         to_plane(q_turn, q_all, tok_row, tok, qkv_s.at[0, j], qkv_r.at[0, j], j)
         for j in range(1, part)
     ]
-    q_all[pl.ds(pl.multiple_of(tok_row, 16), tok), :] = q_turn[:, columns(member)]
-    own_kv = pl.ds(pl.multiple_of(HALO + tok_row, 16), tok)
+    q_all[own_row, :] = q_turn[:, columns(member)]
     k_all[own_kv, :] = k_turn[:, columns(member)]
-    v_all[own_kv, :] = v_ref[:, columns(member)]
+    local[2].wait()
+    if n_line > 1:
+        forward(2)
 
     for copy in moved:
         copy.wait_recv()
@@ -171,6 +226,24 @@
         k_all[pl.ds(0, HALO), :] = jnp.zeros((HALO, cols), jnp.bfloat16)
         v_all[pl.ds(0, HALO), :] = jnp.zeros((HALO, cols), jnp.bfloat16)
 
+    for d in range(3, n_line + 1):
+        forward(d)
+
+    def table(b, carry):
+        queries = (line * part + b) * tok + lax.broadcasted_iota(jnp.int32, (tok, 1), 0)
+        near = (line * part + b) * tok - HALO + lax.broadcasted_iota(jnp.int32, (1, span), 1)
+        _, begins, owners, nears = lax.fori_loop(
+            0, requests, lambda r, state: request(r, state, queries, near),
+            (jnp.int32(0), zero, zero, jnp.zeros((1, span), jnp.int32)),
+        )
+        row = pl.ds(pl.multiple_of(b * tok, 16), tok)
+        begin[row, :] = begins
+        group_of[row, :] = owners
+        near_begin[b] = nears
+        return carry
+
+    lax.fori_loop(0, part, table, 0)
+
     for copy in moved_q:
         copy.wait_recv()
 
@@ -179,10 +252,6 @@
         for copy in halos:
             copy.wait_recv()
 
-    for copy in lines:
-        copy.wait_recv()
-
-    span = HALO + tok
     factor = math.log2(math.e) / math.sqrt(HD)
     later = lax.broadcasted_iota(jnp.int32, (tok, span), 1) - HALO <= lax.broadcasted_iota(
         jnp.int32, (tok, span), 0
@@ -201,8 +270,8 @@
         b = (member + step) % part
         row = pl.ds(pl.multiple_of(b * tok, 16), tok)
         window = pl.ds(pl.multiple_of(b * tok, 16), span)
-        group = qg_ref[row, :]
-        allowed = (ks_ref[b] == qs_ref[row, :]) & later
+        group = group_of[row, :]
+        allowed = (near_begin[b] == begin[row, :]) & later
         for h in range(cols // HD):
             at = slice(h * HD, (h + 1) * HD)
             q = q_all[row, at]
@@ -265,21 +334,20 @@
     @pl.loop(0, out_w // TILE)
     def _(t):
         at = pl.ds(pl.multiple_of(t * TILE, TILE), TILE)
-        own[:, at] = project(head * out_w, t)
+        own[:, at] = project(head * out_w, t).astype(jnp.bfloat16)
 
     for copy in sums:
         copy.wait_recv()
 
-    @pl.loop(0, out_w // TILE)
-    def _(t):
-        at = pl.ds(pl.multiple_of(t * TILE, TILE), TILE)
-        whole = own[:, at]
-        for j in range(1, n_heads):
-            whole += take[j - 1, :, at].astype(jnp.float32)
-        out_ref[:, at] = whole.astype(jnp.bfloat16)
-
-    for copy in pre + moved + lines + moved_q + sums:
+    for copy in pre + moved + moved_q + sums:
         copy.wait_send()
+    for d in range(1, n_line):
+        for i in range(2):
+            for sign in (1, -1):
+                @pl.when(sends(sign, d))
+                def _():
+                    hop(sign, i, d).wait_send()
+
     for step in range(1, part):
         send_back(step).wait_send()
 
@@ -299,28 +367,21 @@
     cols = width // part
     n_pre = rows_pre * n_blk
     out_w = out_weight.shape[1] // n_heads
-    blk = lax.axis_index("blk")
-    first = blk // part * (part * tok)
-    plane = first + jnp.arange(part * tok, dtype=jnp.int32)
-    start, group = request_tables(lengths, groups, plane)
-    window = (
-        first - HALO
-        + jnp.arange(part, dtype=jnp.int32)[:, None, None] * tok
-        + jnp.arange(HALO + tok, dtype=jnp.int32)[None, None, :]
-    )
-    near_start = request_tables(lengths, groups, window)[0]
-    mine = blk * tok + jnp.arange(tok, dtype=jnp.int32)
-    position = n_pre // GROUPS + mine - request_tables(lengths, groups, mine)[0]
-    tables = rotary_tables(position)
     vmem = pl.BlockSpec(memory_space=pltpu.VMEM)
+    smem = pl.BlockSpec(memory_space=pltpu.SMEM)
     bf = jnp.bfloat16
     dma = pltpu.SemaphoreType.DMA
-    return pl.pallas_call(
+    own, others = pl.pallas_call(
         functools.partial(kernel, part, n_line, n_heads),
-        out_shape=jax.ShapeDtypeStruct((tok, out_w), bf),
-        in_specs=[vmem] * 9 + [pl.BlockSpec(memory_space=pl.ANY)],
-        out_specs=vmem,
+        out_shape=(
+            jax.ShapeDtypeStruct((tok, out_w), bf),
+            jax.ShapeDtypeStruct((n_heads - 1, tok, out_w), bf),
+        ),
+        in_specs=[smem, smem, vmem] + [pl.BlockSpec(memory_space=pl.ANY)] * 6,
+        out_specs=(vmem, vmem),
         scratch_shapes=[
+            pltpu.VMEM((tok, width), bf),
+            pltpu.VMEM((tok, width), bf),
             pltpu.VMEM((tok, width), bf),
             pltpu.VMEM((tok, width), bf),
             pltpu.VMEM((part * tok, cols), bf),
@@ -332,23 +393,28 @@
             pltpu.VMEM((tok, width), bf),
             pltpu.VMEM(out_weight.shape, bf),
             pltpu.VMEM((n_heads - 1, tok, out_w), bf),
-            pltpu.VMEM((n_heads - 1, tok, out_w), bf),
-            pltpu.VMEM((tok, out_w), jnp.float32),
+            pltpu.VMEM((part * tok, 1), jnp.int32),
+            pltpu.VMEM((part * tok, 1), jnp.int32),
+            pltpu.VMEM((part, 1, HALO + tok), jnp.int32),
             dma((2, part)), dma((2, part)),
             dma((3, part)), dma((3, part)),
-            dma((2, n_line)), dma((2, n_line)),
+            dma((2, 2, n_line)), dma((2, 2, n_line)),
             dma((2,)), dma((2,)),
             dma((part,)), dma((part,)),
             dma((n_heads,)), dma((n_heads,)),
-            dma,
+            dma((2,)), dma((3,)), dma,
         ],
         compiler_params=pltpu.CompilerParams(
             collective_id=0, has_side_effects=True, vmem_limit_bytes=56 << 20
         ),
     )(
-        queries, keys, values, prefix_keys, prefix_values, tables,
-        start[:, None], group[:, None], near_start, out_weight,
+        lengths, groups, jnp.asarray(rotary_rates()),
+        queries, keys, values, prefix_keys, prefix_values, out_weight,
     )
+    total = own.astype(jnp.float32)
+    for j in range(n_heads - 1):
+        total += others[j].astype(jnp.float32)
+    return total.astype(bf)
 
 
 def solution(mesh):

time: 96.6 us -> 81.7 us (0.85)
  the two profiles are of different devices: /device:TPU:18 before, /device:TPU:26 now
where the time goes in v2:
time: 81.7 us; the launch traced here: 81.5 us
  Pallas kernels  79 us (97%)
  other arithmetic  2.52 us (3%)
    pallas_call x1, Pallas kernels, body(): pl.pallas_call(functools.partial(kernel, part, n_line, n_heads), out_shap...  79 us
    convert_element_type x1, other arithmetic, body(): return total.astype(bf)  2.52 us

profile of v2, /device:TPU:26, one launch (start us, length us, event | category | flops | bytes accessed | tf_op | source)
XLA Modules:
  0.0 81.5 jit_solution(5462063338940814942)
XLA Ops:
  0.0 79.0 %shard_map.91 = (bf16[192,2048]{1,0:T(8,128)(2,1)}, bf16[1,192,2048]{2,1,0:T(8,128)(2,1)}) custom-call(s32[24]{0:T(128)} %len_ref.1, s32[24]{0:T(128)} %grp_ref.1, f32[1,128]{1,0:T(1,128)} %constant.2.clone.rate_ref, bf16[192,2048]{1,0:T(8,128)(2,1)} %q_ref.1, bf16[192,2048]{1,0:T(8,128)(2,1)} %k_ref.1, bf16[192,2048]{1,0:T(8,128)(2,1)} %v_ref.1, ...), custom_call_target="tpu_custom_call" | custom-call | tf_op jit(solution)/shard_map/pallas_call | solution.py:374
  79.0 2.5 %fusion = bf16[192,2048]{1,0:T(8,128)(2,1)} fusion(bf16[192,2048]{1,0:T(8,128)(2,1)} %get-tuple-element.7, bf16[1,192,2048]{2,1,0:T(8,128)(2,1)} %get-tuple-element.8), kind=kLoop, calls=%fused_computation.1 | loop fusion | flops 1572864 | bytes 2359296 | tf_op jit(solution)/shard_map/convert_element_type | solution.py:417

commit v3 on v2

v3 whole, which is shorter than its diff:
```python
import functools
import math

import jax
import jax.numpy as jnp
import numpy as np
from jax import lax
from jax.experimental import pallas as pl
from jax.experimental.pallas import tpu as pltpu
from jax.sharding import PartitionSpec as P

HD = 128
ROT = 32
GROUPS = 4
MOST = 224
HALO = (MOST - 1 + 15) // 16 * 16
TILE = 256
MESH = pl.DeviceIdType.MESH


def rotary_rates():
    half = ROT // 2
    rates = np.zeros((1, HD), np.float32)
    rates[0, :half] = 10000.0 ** (-(np.arange(half, dtype=np.float32) * np.float32(2.0 / ROT)))
    rates[0, half:ROT] = rates[0, :half]
    return rates


def dot_t(a, b):
    return lax.dot_general(a, b, (((1,), (1,)), ((), ())), preferred_element_type=jnp.float32)


def kernel(
    part, n_line, n_heads,
    len_ref, grp_ref, rate_ref, q_ref, k_ref, v_ref, pk_ref, pv_ref, w_ref,
    own, take,
    q_in, k_in, q_turn, k_turn, q_all, k_all, v_all, pk_all, pv_all, sent, attn, weight, give, acc,
    begin, group_of, near_begin,
    pre_s, pre_r, qkv_s, qkv_r, line_s, line_r, halo_s, halo_r, back_s, back_r, sum_s, sum_r,
    in_sem, own_sem, w_sem,
):
    tok, width = q_ref.shape
    cols = width // part
    rows_pre = pk_ref.shape[0]
    chunks = len(pk_all)
    n_pre, some = pk_all[0].shape
    prefix_len = n_pre // GROUPS
    out_w = own.shape[1]
    requests = len_ref.shape[0]
    span = HALO + tok
    blk = lax.axis_index("blk")
    head = lax.axis_index("heads")
    line = blk // part
    member = blk % part
    base = line * part

    fetch = [
        pltpu.make_async_copy(
            w_ref.at[pl.ds(m * cols + c * some, some), :],
            weight[c].at[pl.ds(m * some, some), :], w_sem.at[c, m],
        )
        for c in range(chunks)
        for m in range(part)
    ]
    loads = [
        pltpu.make_async_copy(k_ref, k_in, in_sem.at[0]),
        pltpu.make_async_copy(q_ref, q_in, in_sem.at[1]),
    ]
    for copy in loads:
        copy.start()

    barrier = pltpu.get_barrier_semaphore()
    for j in range(1, part):
        pl.semaphore_signal(
            barrier, inc=1, device_id={"blk": base + (member + j) % part}, device_id_type=MESH
        )
    for j in range(1, n_line):
        pl.semaphore_signal(
            barrier, inc=1, device_id={"blk": (line + j) % n_line * part + member},
            device_id_type=MESH,
        )
    for j in range(1, n_heads):
        pl.semaphore_signal(
            barrier, inc=1, device_id={"heads": (head + j) % n_heads}, device_id_type=MESH
        )
    pl.semaphore_wait(barrier, part + n_line + n_heads - 3)

    def columns(m, c):
        return pl.ds(pl.multiple_of(m * cols + c * some, some), some)

    def to_plane(src, dst, c, row, rows, send, recv, j):
        peer = (member + j) % part
        copy = pltpu.make_async_remote_copy(
            src_ref=src.at[:, columns(peer, c)],
            dst_ref=dst[c].at[pl.ds(pl.multiple_of(row, 16), rows), :],
            send_sem=send, recv_sem=recv,
            device_id={"blk": base + peer}, device_id_type=MESH,
        )
        copy.start()
        return copy

    pre_row = blk * rows_pre
    tok_row = member * tok
    pre = [
        [
            to_plane(src, dst, c, pre_row, rows_pre, pre_s.at[i, c, j], pre_r.at[i, c, j], j)
            for i, (src, dst) in enumerate(((pk_ref, pk_all), (pv_ref, pv_all)))
            for j in range(1, part)
        ]
        for c in range(chunks)
    ]

    def move(i, src, dst, first, c):
        return [
            to_plane(src, dst, c, first + tok_row, tok, qkv_s.at[i, c, j], qkv_r.at[i, c, j], j)
            for j in range(1, part)
        ]

    moved = [move(2, v_ref, v_all, HALO, 0)] + [[] for _ in range(chunks - 1)]
    own_pre = pl.ds(pl.multiple_of(pre_row, 16), rows_pre)
    own_row = pl.ds(pl.multiple_of(tok_row, 16), tok)
    own_kv = pl.ds(pl.multiple_of(HALO + tok_row, 16), tok)
    local = [
        pltpu.make_async_copy(
            src.at[:, columns(member, c)], dst[c].at[rows, :], own_sem.at[i, c]
        )
        for i, (src, dst, rows) in enumerate(
            ((pk_ref, pk_all, own_pre), (pv_ref, pv_all, own_pre), (v_ref, v_all, own_kv))
        )
        for c in range(chunks)
    ]
    for copy in local + fetch:
        copy.start()

    def request(r, state, queries, near):
        start, begins, owners, nears = state
        length = len_ref[r]
        end = start + length
        inside = (queries >= start) & (queries < end)
        begins = jnp.where(inside, start + 1, begins)
        if owners is not None:
            owners = jnp.where(inside, grp_ref[r], owners)
        if nears is not None:
            nears = jnp.where((near >= start) & (near < end), start + 1, nears)
        return end, begins, owners, nears

    index = blk * tok + lax.broadcasted_iota(jnp.int32, (tok, 1), 0)
    zero = jnp.zeros((tok, 1), jnp.int32)
    mine = lax.fori_loop(
        0, requests, lambda r, state: request(r, state, index, None),
        (jnp.int32(0), zero, None, None),
    )[1]
    position = prefix_len + index + 1 - mine
    angle = position.astype(jnp.float32) * rate_ref[...]
    lane = lax.broadcasted_iota(jnp.int32, (tok, HD), 1)
    same, sine = jnp.cos(angle), jnp.sin(angle)
    below = jnp.where(lane < ROT // 2, -sine, 0.0)
    above = jnp.where(lane < ROT // 2, 0.0, sine)

    def turn(src, dst):
        for h in range(width // HD):
            at = slice(h * HD, (h + 1) * HD)
            x = src[:, at].astype(jnp.float32)
            y = x * same + pltpu.roll(x, HD - ROT // 2, 1) * below + pltpu.roll(x, ROT // 2, 1) * above
            dst[:, at] = y.astype(jnp.bfloat16)

    loads[0].wait()
    turn(k_in, k_turn)
    moved[0] += move(1, k_turn, k_all, HALO, 0)
    shard = part * rows_pre

    def hop(sign, i, c, d):
        ref = (pk_all, pv_all)[i]
        side = (sign + 1) // 2
        away = lax.rem(line - sign * (d - 1) + n_line, n_line)
        rows = pl.ds(pl.multiple_of(away * shard, 16), shard)
        return pltpu.make_async_remote_copy(
            src_ref=ref[c].at[rows, :], dst_ref=ref[c].at[rows, :],
            send_sem=line_s.at[side, i, c, d], recv_sem=line_r.at[side, i, c, d],
            device_id={"blk": lax.rem(line + sign + n_line, n_line) * part + member},
            device_id_type=MESH,
        )

    def sends(sign, d):
        if sign > 0:
            return (line >= d - 1) & (line < n_line - 1)
        return (line < n_line - d + 1) & (line > 0)

    def receives(sign, d):
        return line >= d if sign > 0 else line < n_line - d

    def forward(c, d):
        for i in range(2):
            for sign in (1, -1):
                if d > 1:
                    @pl.when(receives(sign, d - 1))
                    def _():
                        hop(sign, i, c, d - 1).wait_recv()

                if d < n_line:
                    @pl.when(sends(sign, d))
                    def _():
                        hop(sign, i, c, d).start()

    for copy in local:
        copy.wait()
    for copy in pre[0]:
        copy.wait_recv()
    forward(0, 1)
    loads[1].wait()
    turn(q_in, q_turn)
    moved_q = [move(0, q_turn, q_all, 0, 0)]
    for c in range(1, chunks):
        moved[c] += move(2, v_ref, v_all, HALO, c)
        moved[c] += move(1, k_turn, k_all, HALO, c)
        moved_q.append(move(0, q_turn, q_all, 0, c))
    for c in range(chunks):
        q_all[c][own_row, :] = q_turn[:, columns(member, c)]
        k_all[c][own_kv, :] = k_turn[:, columns(member, c)]

    halos = [
        [
            pltpu.make_async_remote_copy(
                src_ref=ref[c].at[pl.ds(part * tok, HALO), :],
                dst_ref=ref[c].at[pl.ds(0, HALO), :],
                send_sem=halo_s.at[i, c], recv_sem=halo_r.at[i, c],
                device_id={"blk": (line + 1) % n_line * part + member}, device_id_type=MESH,
            )
            for i, ref in enumerate((k_all, v_all))
        ]
        for c in range(chunks)
    ]

    def send_halo(c):
        for copy in moved[c]:
            copy.wait_recv()

        @pl.when(line < n_line - 1)
        def _():
            for copy in halos[c]:
                copy.start()

        @pl.when(line == 0)
        def _():
            k_all[c][pl.ds(0, HALO), :] = jnp.zeros((HALO, some), jnp.bfloat16)
            v_all[c][pl.ds(0, HALO), :] = jnp.zeros((HALO, some), jnp.bfloat16)

    def arrive(c):
        for copy in moved_q[c]:
            copy.wait_recv()

        @pl.when(line > 0)
        def _():
            for copy in halos[c]:
                copy.wait_recv()

    def table(b, carry):
        queries = (line * part + b) * tok + lax.broadcasted_iota(jnp.int32, (tok, 1), 0)
        near = (line * part + b) * tok - HALO + lax.broadcasted_iota(jnp.int32, (1, span), 1)
        _, begins, owners, nears = lax.fori_loop(
            0, requests, lambda r, state: request(r, state, queries, near),
            (jnp.int32(0), zero, zero, jnp.zeros((1, span), jnp.int32)),
        )
        row = pl.ds(pl.multiple_of(b * tok, 16), tok)
        begin[row, :] = begins
        group_of[row, :] = owners
        near_begin[b] = nears
        return carry

    factor = math.log2(math.e) / math.sqrt(HD)
    later = lax.broadcasted_iota(jnp.int32, (tok, span), 1) - HALO <= lax.broadcasted_iota(
        jnp.int32, (tok, span), 0
    )

    def send_back(c, step):
        peer = (member + step) % part
        row = pl.ds(pl.multiple_of(peer * tok, 16), tok)
        return pltpu.make_async_remote_copy(
            src_ref=sent[c].at[row, :],
            dst_ref=attn[c].at[:, pl.ds(pl.multiple_of(member * some, some), some)],
            send_sem=back_s.at[c, step], recv_sem=back_r.at[c, step],
            device_id={"blk": base + peer}, device_id_type=MESH,
        )

    def block(c, step, carry):
        b = (member + step) % part
        row = pl.ds(pl.multiple_of(b * tok, 16), tok)
        window = pl.ds(pl.multiple_of(b * tok, 16), span)
        group = group_of[row, :]
        allowed = (near_begin[b] == begin[row, :]) & later
        for h in range(some // HD):
            at = slice(h * HD, (h + 1) * HD)
            q = q_all[c][row, at]
            near = jnp.where(allowed, dot_t(q, k_all[c][window, at]), -1e30)
            far = dot_t(q, pk_all[c][0:prefix_len, at])
            for g in range(1, GROUPS):
                far = jnp.where(
                    group == g, dot_t(q, pk_all[c][g * prefix_len:(g + 1) * prefix_len, at]), far
                )
            top = jnp.maximum(
                jnp.max(near, axis=1, keepdims=True), jnp.max(far, axis=1, keepdims=True)
            )
            e_near = jnp.exp2((near - top) * factor)
            e_far = jnp.exp2((far - top) * factor)
            total = jnp.sum(e_near, axis=1, keepdims=True) + jnp.sum(e_far, axis=1, keepdims=True)
            acc = jnp.dot(
                e_near.astype(jnp.bfloat16), v_all[c][window, at], preferred_element_type=jnp.float32
            )
            for g in range(GROUPS):
                acc += jnp.dot(
                    jnp.where(group == g, e_far, 0.0).astype(jnp.bfloat16),
                    pv_all[c][g * prefix_len:(g + 1) * prefix_len, at],
                    preferred_element_type=jnp.float32,
                )
            sent[c][row, at] = (acc / total).astype(jnp.bfloat16)

        @pl.when(step < part)
        def _():
            send_back(c, step).start()

        return carry

    def attend(c):
        lax.fori_loop(1, part + 1, functools.partial(block, c), 0)
        attn[c][:, pl.ds(pl.multiple_of(member * some, some), some)] = sent[c][own_row, :]

    def returned(c):
        for step in range(1, part):
            send_back(c, step).wait_recv()
        for copy in fetch[c * part:(c + 1) * part]:
            copy.wait()

    def project(c, at):
        return jnp.dot(attn[c][...], weight[c][:, at], preferred_element_type=jnp.float32)

    def tile(first, t):
        return pl.ds(pl.multiple_of(first + t * TILE, TILE), TILE)

    def gather(c):
        for d in range(2, n_line + 1):
            forward(c, d)
            if d == 2 and c + 1 < chunks:
                for copy in pre[c + 1]:
                    copy.wait_recv()
                forward(c + 1, 1)
            if d == 2 or n_line == 2:
                send_halo(c)
                if c == 0:
                    lax.fori_loop(0, part, table, 0)

    gather(0)
    arrive(0)
    attend(0)
    for c in range(1, chunks):
        gather(c)
        returned(c - 1)

        @pl.loop(0, n_heads * out_w // TILE)
        def _(t):
            at = tile(0, t)
            if c == 1:
                acc[:, at] = project(c - 1, at)
            else:
                acc[:, at] += project(c - 1, at)

        arrive(c)
        attend(c)
    returned(chunks - 1)

    def final(at):
        value = project(chunks - 1, at)
        return value + acc[:, at] if chunks > 1 else value

    sums = []
    for j in range(1, n_heads):
        peer = (head + j) % n_heads

        @pl.loop(0, out_w // TILE)
        def _(t):
            give[j - 1, :, tile(0, t)] = final(tile(peer * out_w, t)).astype(jnp.bfloat16)

        copy = pltpu.make_async_remote_copy(
            src_ref=give.at[j - 1], dst_ref=take.at[j - 1],
            send_sem=sum_s.at[j], recv_sem=sum_r.at[j],
            device_id={"heads": peer}, device_id_type=MESH,
        )
        copy.start()
        sums.append(copy)

    @pl.loop(0, out_w // TILE)
    def _(t):
        own[:, tile(0, t)] = final(tile(head * out_w, t)).astype(jnp.bfloat16)

    for copy in sums:
        copy.wait_recv()

    for copy in sum(pre + moved + moved_q, []) + sums:
        copy.wait_send()
    for c in range(chunks):
        for d in range(1, n_line):
            for i in range(2):
                for sign in (1, -1):
                    @pl.when(sends(sign, d))
                    def _():
                        hop(sign, i, c, d).wait_send()

        for step in range(1, part):
            send_back(c, step).wait_send()

        @pl.when(line < n_line - 1)
        def _():
            for copy in halos[c]:
                copy.wait_send()


def body(queries, keys, values, prefix_keys, prefix_values, lengths, groups, out_weight):
    tok, width = queries.shape
    rows_pre = prefix_keys.shape[0]
    n_blk = lax.axis_size("blk")
    n_heads = lax.axis_size("heads")
    part = math.gcd(4, math.gcd(width // HD, n_blk))
    n_line = n_blk // part
    cols = width // part
    chunks = math.gcd(2, cols // HD)
    some = cols // chunks
    n_pre = rows_pre * n_blk
    out_w = out_weight.shape[1] // n_heads
    vmem = pl.BlockSpec(memory_space=pltpu.VMEM)
    smem = pl.BlockSpec(memory_space=pltpu.SMEM)
    bf = jnp.bfloat16
    dma = pltpu.SemaphoreType.DMA
    own, others = pl.pallas_call(
        functools.partial(kernel, part, n_line, n_heads),
        out_shape=(
            jax.ShapeDtypeStruct((tok, out_w), bf),
            jax.ShapeDtypeStruct((n_heads - 1, tok, out_w), bf),
        ),
        in_specs=[smem, smem, vmem] + [pl.BlockSpec(memory_space=pl.ANY)] * 6,
        out_specs=(vmem, vmem),
        scratch_shapes=[
            pltpu.VMEM((tok, width), bf),
            pltpu.VMEM((tok, width), bf),
            pltpu.VMEM((tok, width), bf),
            pltpu.VMEM((tok, width), bf),
            [pltpu.VMEM((part * tok, some), bf)] * chunks,
            [pltpu.VMEM((HALO + part * tok, some), bf)] * chunks,
            [pltpu.VMEM((HALO + part * tok, some), bf)] * chunks,
            [pltpu.VMEM((n_pre, some), bf)] * chunks,
            [pltpu.VMEM((n_pre, some), bf)] * chunks,
            [pltpu.VMEM((part * tok, some), bf)] * chunks,
            [pltpu.VMEM((tok, width // chunks), bf)] * chunks,
            [pltpu.VMEM((width // chunks, out_weight.shape[1]), bf)] * chunks,
            pltpu.VMEM((n_heads - 1, tok, out_w), bf),
            pltpu.VMEM((tok, out_weight.shape[1]), jnp.float32),
            pltpu.VMEM((part * tok, 1), jnp.int32),
            pltpu.VMEM((part * tok, 1), jnp.int32),
            pltpu.VMEM((part, 1, HALO + tok), jnp.int32),
            dma((2, chunks, part)), dma((2, chunks, part)),
            dma((3, chunks, part)), dma((3, chunks, part)),
            dma((2, 2, chunks, n_line)), dma((2, 2, chunks, n_line)),
            dma((2, chunks)), dma((2, chunks)),
            dma((chunks, part)), dma((chunks, part)),
            dma((n_heads,)), dma((n_heads,)),
            dma((2,)), dma((3, chunks)), dma((chunks, part)),
        ],
        compiler_params=pltpu.CompilerParams(
            collective_id=0, has_side_effects=True, vmem_limit_bytes=56 << 20
        ),
    )(
        lengths, groups, jnp.asarray(rotary_rates()),
        queries, keys, values, prefix_keys, prefix_values, out_weight,
    )
    total = own.astype(jnp.float32)
    for j in range(n_heads - 1):
        total += others[j].astype(jnp.float32)
    return total.astype(bf)


def solution(mesh):
    placed = (
        P("blk", "heads"),
        P("blk", "heads"),
        P("blk", "heads"),
        P("blk", "heads"),
        P("blk", "heads"),
        P(),
        P(),
        P("heads", None),
    )
    return jax.shard_map(
        body, mesh=mesh, in_specs=placed, out_specs=P("blk", "heads"), check_vma=False
    )
```

time: 81.7 us -> 76.6 us (0.938)
  Pallas kernels: 79 us -> 73.6 us
    pallas_call x1, Pallas kernels: 79 us -> 73.6 us  [body(): pl.pallas_call(functools.partial(kernel, part, n_line, n_heads), out_shap...]
where the time goes in v3:
time: 76.6 us; the launch traced here: 76.1 us
  Pallas kernels  73.6 us (96%)
  other arithmetic  2.52 us (3%)
    pallas_call x1, Pallas kernels, body(): pl.pallas_call(functools.partial(kernel, part, n_line, n_heads), out_shap...  73.6 us
    convert_element_type x1, other arithmetic, body(): return total.astype(bf)  2.52 us

profile of v3, /device:TPU:26, one launch (start us, length us, event | category | flops | bytes accessed | tf_op | source)
XLA Modules:
  0.0 76.1 jit_solution(6310073864798582154)
XLA Ops:
  0.0 73.6 %shard_map.91 = (bf16[192,2048]{1,0:T(8,128)(2,1)}, bf16[1,192,2048]{2,1,0:T(8,128)(2,1)}) custom-call(s32[24]{0:T(128)} %len_ref.1, s32[24]{0:T(128)} %grp_ref.1, f32[1,128]{1,0:T(1,128)} %constant.2.clone.rate_ref, bf16[192,2048]{1,0:T(8,128)(2,1)} %q_ref.1, bf16[192,2048]{1,0:T(8,128)(2,1)} %k_ref.1, bf16[192,2048]{1,0:T(8,128)(2,1)} %v_ref.1, ...), custom_call_target="tpu_custom_call" | custom-call | tf_op jit(solution)/shard_map/pallas_call | solution.py:432
  73.6 2.5 %fusion = bf16[192,2048]{1,0:T(8,128)(2,1)} fusion(bf16[192,2048]{1,0:T(8,128)(2,1)} %get-tuple-element.7, bf16[1,192,2048]{2,1,0:T(8,128)(2,1)} %get-tuple-element.8), kind=kLoop, calls=%fused_computation.1 | loop fusion | flops 1572864 | bytes 2359296 | tf_op jit(solution)/shard_map/convert_element_type | solution.py:476

commit v4 on v3

--- a/solution.py
+++ b/solution.py
@@ -337,16 +337,20 @@
         return pl.ds(pl.multiple_of(first + t * TILE, TILE), TILE)
 
     def gather(c):
-        for d in range(2, n_line + 1):
+        if c == 0:
+            forward(0, 2)
+        if c + 1 < chunks:
+            for copy in pre[c + 1]:
+                copy.wait_recv()
+            forward(c + 1, 1)
+        if c == 0:
+            send_halo(0)
+            lax.fori_loop(0, part, table, 0)
+        for d in range(3, n_line + 1):
             forward(c, d)
-            if d == 2 and c + 1 < chunks:
-                for copy in pre[c + 1]:
-                    copy.wait_recv()
-                forward(c + 1, 1)
-            if d == 2 or n_line == 2:
-                send_halo(c)
-                if c == 0:
-                    lax.fori_loop(0, part, table, 0)
+        if c + 1 < chunks:
+            forward(c + 1, 2)
+            send_halo(c + 1)
 
     gather(0)
     arrive(0)

time: 76.6 us -> 76.1 us (level)
  no operation moved by 1% of the time
where the time goes in v4:
time: 76.1 us; the launch traced here: 75.8 us
  Pallas kernels  73.2 us (96%)
  other arithmetic  2.52 us (3%)
    pallas_call x1, Pallas kernels, body(): pl.pallas_call(functools.partial(kernel, part, n_line, n_heads), out_shap...  73.2 us
    convert_element_type x1, other arithmetic, body(): return total.astype(bf)  2.52 us

profile of v4, /device:TPU:26, one launch (start us, length us, event | category | flops | bytes accessed | tf_op | source)
XLA Modules:
  0.0 75.8 jit_solution(8417921166709896796)
XLA Ops:
  0.0 73.2 %shard_map.91 = (bf16[192,2048]{1,0:T(8,128)(2,1)}, bf16[1,192,2048]{2,1,0:T(8,128)(2,1)}) custom-call(s32[24]{0:T(128)} %len_ref.1, s32[24]{0:T(128)} %grp_ref.1, f32[1,128]{1,0:T(1,128)} %constant.2.clone.rate_ref, bf16[192,2048]{1,0:T(8,128)(2,1)} %q_ref.1, bf16[192,2048]{1,0:T(8,128)(2,1)} %k_ref.1, bf16[192,2048]{1,0:T(8,128)(2,1)} %v_ref.1, ...), custom_call_target="tpu_custom_call" | custom-call | tf_op jit(solution)/shard_map/pallas_call | solution.py:436
  73.2 2.5 %fusion = bf16[192,2048]{1,0:T(8,128)(2,1)} fusion(bf16[192,2048]{1,0:T(8,128)(2,1)} %get-tuple-element.7, bf16[1,192,2048]{2,1,0:T(8,128)(2,1)} %get-tuple-element.8), kind=kLoop, calls=%fused_computation.1 | loop fusion | flops 1572864 | bytes 2359296 | tf_op jit(solution)/shard_map/convert_element_type | solution.py:480
